TPU v7x, 1024 devices: a whole 4x8x16 slice. The times are simulated.
1024 devices in a mesh: dp: 16 (over y, core), section: 4 (over x), ctx: 16 (over z).
Axes of the slice: x: 4, y: 8, z: 16, core: 2. Of those that a mesh axis runs over, the one named last changes fastest.
Arguments:
- queries: bfloat16 [4, 16, 2048, 4096], P('section', 'dp', 'ctx'), may hold values from -30 to 30
- keys_values: bfloat16 [4, 16, 2048, 1024], P('section', 'dp', 'ctx'), may hold values from -30 to 30
- random_blocks: int32 [16, 16, 4, 4], P('dp'), may hold values from 0 to 15, as said below
- global_blocks: int32 [16, 2], P('dp'), may hold values from 0 to 15
- doc_lengths: int32 [16, 4], P('dp'), may hold values from 1 to 1024, 2048 in all within a row
- cotangent: bfloat16 [4, 16, 2048, 4096], P('section', 'dp', 'ctx'), may hold values from -1.5 to 1.5
Outputs:
- stream: bfloat16 [4, 16, 2048, 4096], P('section', 'dp', 'ctx')
- gain_grad: float32 [4, 4096], P('section')
Inputs may be any that keep to these rules, and one draw needn't show every extreme that they name: `random_blocks`: for each query block, its 4 x 4 entries over all key heads name every block of the sequence exactly 1 times.
All inputs are finite; a program needn't handle non-finite values.
Results may differ from a plain program's by a relative error of at most 0.0062.
Values may be sent and summed in bfloat16 or wider, within the bound.
A program may use at most 32 MiB of HBM per device.

v0:
```python
import math

import jax
import jax.numpy as jnp
from jax import lax
from jax.sharding import PartitionSpec as P

HEADS = 32
KVH = 4
HD = 128
RAND = 4
GLOBALS = 2
GROUP = 8


def extended(cells, sides, width):
    for axis, dim in sides:
        count = lax.axis_size(axis)
        ends = count - 1
        head = lax.slice_in_dim(cells, 0, width, axis=dim)
        tail = lax.slice_in_dim(cells, cells.shape[dim] - width, cells.shape[dim], axis=dim)
        cells = jnp.concatenate(
            [
                lax.ppermute(tail, axis, [(i, (i + 1) % count) for i in range(ends)]),
                cells,
                lax.ppermute(head, axis, [((i + 1) % count, i) for i in range(ends)]),
            ],
            axis=dim,
        )
    return cells


def spread(value, axis, root):
    mine = lax.axis_index(axis) == root
    return lax.psum(jnp.where(mine, value, jnp.zeros_like(value)), axis)


def passed_along(value, axis, steps):
    count = lax.axis_size(axis)
    initial, last = (max(0, -steps), min(count, count - steps))
    return lax.ppermute(value, axis, [(source, source + steps) for source in range(initial, last)])


def by_heads(row_block):
    row_count = row_block.shape[0]
    split_rows = row_block.reshape(row_count, 2, KVH, HD)
    return jnp.transpose(split_rows, (2, 0, 1, 3)).reshape(KVH, row_count, 2 * HD)


def doc_index(doc_ends, positions):
    return jnp.sum((doc_ends <= positions[..., None]).astype(jnp.int32), axis=-1)


def attend_head(operands):
    query_rows, key_rows, value_rows, allowed = operands
    scores = jnp.einsum(
        "qgd,kd->gqk", query_rows, key_rows, preferred_element_type=jnp.float32
    ) / math.sqrt(HD)
    scores = jnp.where(allowed[None], scores, -1e30)
    row_max = jnp.max(scores, axis=-1, keepdims=True)
    weights = jnp.where(allowed[None], jnp.exp(scores - row_max), 0.0)
    weight_sum = jnp.sum(weights, axis=-1)
    product = jnp.einsum(
        "gqk,kd->qgd", weights.astype(jnp.bfloat16), value_rows, preferred_element_type=jnp.float32
    )
    return product / jnp.transpose(weight_sum)[:, :, None]


def per_device(queries, keys_values, random_blocks, global_blocks, doc_lengths, cotangent):
    ctx_count = lax.axis_size("ctx")
    ctx_place = lax.axis_index("ctx")
    local_kv = keys_values[0, 0]
    block_rows = local_kv.shape[0]
    seq_len = ctx_count * block_rows
    block_table = random_blocks[0]
    own_lists = lax.dynamic_index_in_dim(block_table, ctx_place, 0, keepdims=False)
    globals_ids = global_blocks[0]
    window_kv = extended(local_kv, (("ctx", 0),), block_rows)
    global_pieces = []
    for global_slot in range(GLOBALS):
        global_pieces.append(spread(local_kv, "ctx", globals_ids[global_slot]))
    global_kv = jnp.concatenate(global_pieces, axis=0)
    item_count = KVH * RAND
    slots = item_count // ctx_count
    item_index = jnp.arange(item_count, dtype=jnp.int32)
    earlier = (item_index[:, None] < item_index[None, :]).astype(jnp.int32)
    wanted = (block_table.reshape(ctx_count, item_count) == ctx_place).astype(jnp.int32)
    ranks = jnp.sum(wanted[:, :, None] * earlier[None], axis=1)
    head_of = item_index // RAND
    picked = wanted[:, :, None] * (
        ranks[:, :, None] == jnp.arange(slots, dtype=jnp.int32)[None, None, :]
    )
    send_heads = jnp.sum(picked * head_of[None, :, None], axis=1)
    head_major = by_heads(local_kv)
    outgoing = jnp.take(head_major, send_heads.reshape(-1), axis=0)
    outgoing = outgoing.reshape(ctx_count, slots, block_rows, 2 * HD)
    incoming = lax.all_to_all(outgoing, "ctx", split_axis=0, concat_axis=0, tiled=True)
    own_flat = own_lists.reshape(item_count)
    same_source = (own_flat[:, None] == own_flat[None, :]).astype(jnp.int32)
    own_rank = jnp.sum(same_source * earlier, axis=0)
    source_slot = own_flat * slots + own_rank
    random_kv = jnp.take(
        incoming.reshape(ctx_count * slots, block_rows, 2 * HD), source_slot, axis=0
    )
    random_kv = random_kv.reshape(KVH, RAND * block_rows, 2 * HD)
    shared_kv = by_heads(jnp.concatenate([window_kv, global_kv], axis=0))
    all_kv = jnp.concatenate([shared_kv, random_kv], axis=1)
    row_steps = jnp.arange(block_rows, dtype=jnp.int32)
    window_pos = (ctx_place - 1) * block_rows + jnp.arange(3 * block_rows, dtype=jnp.int32)
    global_pos = (globals_ids[:, None] * block_rows + row_steps[None, :]).reshape(-1)
    shared_pos = jnp.concatenate([window_pos, global_pos])
    random_pos = (own_lists[:, :, None] * block_rows + row_steps).reshape(KVH, -1)
    doc_ends = jnp.cumsum(doc_lengths[0])
    query_doc = doc_index(doc_ends, ctx_place * block_rows + row_steps)
    shared_ok = (shared_pos >= 0) & (shared_pos < seq_len)
    shared_ok = shared_ok[None, :] & (
        doc_index(doc_ends, shared_pos)[None, :] == query_doc[:, None]
    )
    random_ok = doc_index(doc_ends, random_pos)[:, None, :] == query_doc[None, :, None]
    allowed = jnp.concatenate(
        [jnp.broadcast_to(shared_ok[None], (KVH,) + shared_ok.shape), random_ok], axis=2
    )
    query_heads = jnp.transpose(queries[0, 0].reshape(block_rows, KVH, GROUP, HD), (1, 0, 2, 3))
    attention = lax.map(attend_head, (query_heads, all_kv[:, :, :HD], all_kv[:, :, HD:], allowed))
    attention = jnp.transpose(attention, (1, 0, 2, 3)).reshape(block_rows, HEADS * HD)
    rounded_out = attention.astype(jnp.bfloat16)
    section_place = lax.axis_index("section")
    section_count = lax.axis_size("section")
    handed = rounded_out
    for section_step in range(1, section_count):
        arrived = passed_along(handed, "section", 1)
        updated = (arrived.astype(jnp.float32) + rounded_out.astype(jnp.float32)).astype(
            jnp.bfloat16
        )
        handed = jnp.where(section_place == section_step, updated, handed)
    widened = handed.astype(jnp.float32)
    inverse = lax.rsqrt(jnp.mean(widened * widened, axis=-1, keepdims=True) + 1e-06)
    gradient_term = jnp.sum(
        cotangent[0, 0].astype(jnp.float32) * widened * inverse, axis=0
    ) / lax.axis_size("dp")
    gain_grad = lax.psum(gradient_term, ("dp", "ctx"))
    return (handed[None, None], gain_grad[None])


def solution(mesh):
    in_specs = (
        P("section", "dp", "ctx", None),
        P("section", "dp", "ctx", None),
        P("dp", None, None, None),
        P("dp", None),
        P("dp", None),
        P("section", "dp", "ctx", None),
    )
    out_specs = (P("section", "dp", "ctx", None), P("section", None))
    return jax.shard_map(
        per_device, mesh=mesh, in_specs=in_specs, out_specs=out_specs, check_vma=False
    )
```

profile of v0, /device:TPU:7, one launch (start us, length us, event | category | flops | bytes accessed | tf_op | source)
XLA Modules:
  0.0 1270.8 jit_solution(10266732487405488485)
XLA Ops:
  7.2 1.1 copy.92
  8.3 4.7 collective-permute-start
  13.0 1.3 collective-permute-start.1
  14.3 0.7 compare_convert_fusion
  15.2 0.1 multiply_reduce_fusion
  15.3 0.1 multiply_reduce_fusion.1
  15.5 0.7 gather_fusion
  16.2 1.2 fusion.67
  17.4 19.2 %all-to-all-start = ((bf16[16,1,128,256]{2,3,1,0:T(8,128)(2,1)}), bf16[16,1,128,256]{2,3,1,0:T(8,128)(2,1)S(1)}, u32[]{:S(2)}, u32[]{:S(2)}) async-start(bf16[16,1,128,256]{2,3,1,0:T(8,128)(2,1)} %fusion.67), calls=%async_computation | async-start | bytes 2097152 | tf_op jit(solution)/shard_map/all_to_all | solution.py:97
  36.6 0.6 fusion.77
  38.5 0.8 broadcast_select_fusion.1
  39.4 0.2 dynamic-slice_reduce_fusion
  39.6 0.1 reshape.346
  39.7 0.1 select_reduce_fusion
  39.8 0.1 reshape.349
  39.9 0.1 reduce_sum.88
  40.0 0.2 reduce-window.8
  40.2 0.1 add_bitcast_fusion
  40.3 0.1 convert_reduce_fusion.2
  40.4 0.1 convert_reduce_fusion.1
  40.5 0.1 convert_reduce_fusion
  40.7 0.1 broadcast_bitcast_fusion.1
  40.7 0.2 compare_and_fusion
  41.0 0.3 broadcast_compare_fusion
  41.3 0.1 broadcast_in_dim.95
  41.4 0.9 pad_add_fusion
  42.3 1.3 copy.101
  43.7 1.7 constant_dynamic-update-slice_fusion.4
  45.4 0.8 constant_dynamic-update-slice_fusion.3
  46.1 0.8 constant_dynamic-update-slice_fusion.2
  46.9 140.2 %all-reduce.3.cloned.1.call-done = (bf16[128,2,4,128]{0,3,2,1:T(8,128)(2,1)}, bf16[128,2,4,128]{0,3,2,1:T(8,128)(2,1)}) async-done(((bf16[128,2,4,128]{0,3,2,1:T(8,128)(2,1)}, bf16[128,2,4,128]{0,3,2,1:T(8,128)(2,1)}), (bf16[128,2,4,128]{0,3,2,1:T(8,128)(2,1)}, bf16[128,2,4,128]{0,3,2,1:T(8,128)(2,1)})) %all-reduce.3.cloned.1.call-update) | async-done | bytes 524304 | tf_op jit(solution)/shard_map/psum | solution.py:35
  187.1 1.7 constant_dynamic-update-slice_fusion.1
  188.8 1.7 constant_dynamic-update-slice_fusion
  190.5 1.4 copy.94
  192.0 0.5 copy.99
  192.5 0.6 gather_fusion.1
  193.1 0.5 copy.100
  193.7 0.1 broadcast_select_fusion
  193.8 1.3 pad_maximum_fusion
  195.1 27.0 %while.10 = (s32[]{:T(128)}, bf16[4,128,8,128]{1,3,2,0:T(8,128)(2,1)}, bf16[4,1152,128]{1,2,0:T(8,128)(2,1)}, pred[4,128,1152]{1,2,0:T(8,128)(4,1)}, bf16[4,1152...) while((s32[]{:T(128)}, bf16[4,128,8,128]{1,3,2,0:T(8,128)(2,1)}, ...), condition=%wide.region_12.13_spmd, body=%wide.region_9.12_spmd.sunk | while | flops 917900544 | bytes 2829393 | solution.py:124
  195.1 0.9 dynamic-slice_bitcast_fusion.2
  196.0 2.1 fusion.92
  198.1 3.8 fusion.93
  201.9 0.9 dynamic-slice_bitcast_fusion.2
  202.8 2.1 fusion.92
  204.9 3.8 fusion.93
  208.6 0.9 dynamic-slice_bitcast_fusion.2
  209.5 2.1 fusion.92
  211.6 3.8 fusion.93
  215.4 0.9 dynamic-slice_bitcast_fusion.2
  216.3 2.1 fusion.92
  218.4 3.8 fusion.93
  222.1 1.5 copy.106
  223.6 1.3 collective-permute-start.2
  224.9 14.9 %collective-permute-done.2 = bf16[128,4096]{1,0:T(8,128)(2,1)S(1)} collective-permute-done((bf16[128,4096]{1,0:T(8,128)(2,1)S(1)}, bf16[128,4096]{1,0:T(8,128)(2,1)S(1)}, u32[]{:S(2)}, u32[]{:S(2)}) %collective-permute-start.2) | collective-permute-done | bytes 1048608 | tf_op jit(solution)/shard_map/ppermute | solution.py:41
  239.8 0.3 fusion.63
  240.1 1.3 collective-permute-start.3
  241.4 20.3 %collective-permute-done.3 = bf16[128,4096]{1,0:T(8,128)(2,1)} collective-permute-done((bf16[128,4096]{1,0:T(8,128)(2,1)S(1)}, bf16[128,4096]{1,0:T(8,128)(2,1)}, u32[]{:S(2)}, u32[]{:S(2)}) %collective-permute-start.3) | collective-permute-done | bytes 1048608 | tf_op jit(solution)/shard_map/ppermute | solution.py:41
  261.7 1.7 fusion.66
  263.4 1.3 collective-permute-start.4
  264.8 19.9 %collective-permute-done.4 = bf16[128,4096]{1,0:T(8,128)(2,1)} collective-permute-done((bf16[128,4096]{1,0:T(8,128)(2,1)S(1)}, bf16[128,4096]{1,0:T(8,128)(2,1)}, u32[]{:S(2)}, u32[]{:S(2)}) %collective-permute-start.4) | collective-permute-done | bytes 1048608 | tf_op jit(solution)/shard_map/ppermute | solution.py:41
  284.6 1.8 fusion.59
  286.5 0.4 fusion.58
  286.9 977.1 %psum.23 = f32[1,4096]{1,0:T(1,128)} all-reduce(f32[1,4096]{1,0:T(1,128)S(1)} %bitcast.163), channel_id=1, replica_groups=mesh['dp'=16,'section'=4,'ctx'=16] {'dp','ctx'}, use_global_device_ids=true, to_apply=%region_15.16 | all-reduce | flops 4096 | bytes 32768 | tf_op jit(solution)/shard_map/psum | solution.py:141
  (43 shorter events, 0.5 us)
Async XLA Ops:
  8.3 35.4 %collective-permute-start = (bf16[128,1024]{0,1:T(8,128)(2,1)S(1)}, bf16[128,1024]{0,1:T(8,128)(2,1)}, u32[]{:S(2)}, u32[]{:S(2)}) collective-permute-start(bf16[128,1024]{0,1:T(8,128)(2,1)S(1)} %bitcast.153), channel_id=1, source_target_pairs={{0,1},{1,2},{2,3},{3,4},{4,5},{5,6},{6,7},{7,8},{8,9},{9,10},{10,1... | collective-permute-start | bytes 786440 | tf_op jit(solution)/shard_map/ppermute | solution.py:24
  13.0 33.1 %collective-permute-start.1 = (bf16[128,1024]{0,1:T(8,128)(2,1)S(1)}, bf16[128,1024]{0,1:T(8,128)(2,1)S(1)}, u32[]{:S(2)}, u32[]{:S(2)}) collective-permute-start(bf16[128,1024]{0,1:T(8,128)(2,1)S(1)} %bitcast.154), channel_id=1, source_target_pairs={{1,0},{2,1},{3,2},{4,3},{5,4},{6,5},{7,6},{8,7},{9,8},{10,9},{11,1... | collective-permute-start | bytes 786440 | tf_op jit(solution)/shard_map/ppermute | solution.py:26
  17.4 19.3 %copy-start.5 = (s32[1,2]{1,0:T(1,128)S(1)}, s32[1,2]{1,0:T(1,128)}, u32[]{:S(2)}) copy-start(s32[1,2]{1,0:T(1,128)} %param.11) | copy-start | bytes 28
  17.4 22.0 %copy-start.4 = (s32[1,16,4,4]{1,3,2,0:T(4,128)S(1)}, s32[1,16,4,4]{1,3,2,0:T(4,128)}, u32[]{:S(2)}) copy-start(s32[1,16,4,4]{1,3,2,0:T(4,128)} %param.10) | copy-start | bytes 3076
  17.4 22.6 %copy-start.6 = (s32[1,4]{1,0:T(1,128)S(1)}, s32[1,4]{1,0:T(1,128)}, u32[]{:S(2)}) copy-start(s32[1,4]{1,0:T(1,128)} %param.12) | copy-start | bytes 52
  17.4 174.6 %all-to-all-start = ((bf16[16,1,128,256]{2,3,1,0:T(8,128)(2,1)}), bf16[16,1,128,256]{2,3,1,0:T(8,128)(2,1)S(1)}, u32[]{:S(2)}, u32[]{:S(2)}) async-start(bf16[16,1,128,256]{2,3,1,0:T(8,128)(2,1)} %fusion.67), calls=%async_computation | async-start | bytes 2097152 | tf_op jit(solution)/shard_map/all_to_all | solution.py:97
  36.6 150.5 %all-reduce.3.cloned.1.call-start = ((), (), s32[]{:S(2)}) async-start(), calls=%async_computation.1 | async-start | bytes 1048576 | tf_op jit(solution)/shard_map/psum | solution.py:35
  39.4 3.0 copy-start.2
  193.8 1.3 copy-start.3
  223.6 16.2 %collective-permute-start.2 = (bf16[128,4096]{1,0:T(8,128)(2,1)S(1)}, bf16[128,4096]{1,0:T(8,128)(2,1)S(1)}, u32[]{:S(2)}, u32[]{:S(2)}) collective-permute-start(bf16[128,4096]{1,0:T(8,128)(2,1)S(1)} %copy.106), channel_id=1, source_target_pairs={{0,16},{16,32},{32,48},{1,17},{17,33},{33,49},{2,18},{18,34},{34,5... | collective-permute-start | bytes 3145736 | tf_op jit(solution)/shard_map/ppermute | solution.py:41
  240.1 21.6 %collective-permute-start.3 = (bf16[128,4096]{1,0:T(8,128)(2,1)S(1)}, bf16[128,4096]{1,0:T(8,128)(2,1)}, u32[]{:S(2)}, u32[]{:S(2)}) collective-permute-start(bf16[128,4096]{1,0:T(8,128)(2,1)S(1)} %fusion.63), channel_id=1, source_target_pairs={{0,16},{16,32},{32,48},{1,17},{17,33},{33,49},{2,18},{18,34},{34,5... | collective-permute-start | bytes 3145736 | tf_op jit(solution)/shard_map/ppermute | solution.py:41
  263.4 21.2 %collective-permute-start.4 = (bf16[128,4096]{1,0:T(8,128)(2,1)S(1)}, bf16[128,4096]{1,0:T(8,128)(2,1)}, u32[]{:S(2)}, u32[]{:S(2)}) collective-permute-start(bf16[128,4096]{1,0:T(8,128)(2,1)S(1)} %fusion.66), channel_id=1, source_target_pairs={{0,16},{16,32},{32,48},{1,17},{17,33},{33,49},{2,18},{18,34},{34,5... | collective-permute-start | bytes 3145736 | tf_op jit(solution)/shard_map/ppermute | solution.py:41
  264.7 21.7 %copy-start.1 = (bf16[1,1,128,4096]{3,2,1,0:T(8,128)(2,1)S(1)}, bf16[1,1,128,4096]{3,2,1,0:T(8,128)(2,1)}, u32[]{:S(2)}) copy-start(bf16[1,1,128,4096]{3,2,1,0:T(8,128)(2,1)} %param.13) | copy-start | bytes 3145732
  286.5 977.5 %copy-start = (bf16[128,4096]{1,0:T(8,128)(2,1)}, bf16[128,4096]{1,0:T(8,128)(2,1)S(1)}, u32[]{:S(2)}) copy-start(bf16[128,4096]{1,0:T(8,128)(2,1)S(1)} %get-tuple-element.98) | copy-start | bytes 3145732
Sparse Core Ops, SparseCore 0:
  39.8 147.2 all-reduce.2
where the time goes:
time: 1290 us; the launch traced here: 1270 us
  blocking collectives  977 us (76%)
  waiting for transfers between devices  195 us (15%)
  starting transfers between devices  29.1 us (2%)
  matrix products  23.3 us (2%)
  local copies, waits for them, and re-layouts  19.6 us (2%)
  between operations  15.7 us (1%)
    psum x1, blocking collectives, per_device(): gain_grad = lax.psum(gradient_term, ('dp', 'ctx'))  977 us
    psum x1, waiting for transfers between devices, spread(): return lax.psum(jnp.where(mine, value, jnp.zeros_like(value)), axis)  140 us
    ppermute x3, waiting for transfers between devices, passed_along(): lax.ppermute(value, axis, [(source, source + steps) for source in range(i...  55.1 us
  transfers between devices with their start and end apart: 7, of which 4 were waited for; matrix products, arithmetic and copies ran while one was open for 1% of the time, Pallas kernels for 0%

commit v1 on v0

v1 whole, which is shorter than its diff:
```python
import functools
import math

import jax
import jax.numpy as jnp
from jax import lax
from jax.experimental import pallas as pl
from jax.experimental.pallas import tpu as pltpu
from jax.sharding import PartitionSpec as P

HEADS = 32
KVH = 4
HD = 128
RAND = 4
GLOBALS = 2
GROUP = 8
DOCS = 4
BLOCK = 128
LISTED = 3 + GLOBALS + RAND
PAIRS = HEADS // 2
MESH = pl.DeviceIdType.MESH
FACTOR = math.log2(math.e) / math.sqrt(HD)
LAG = 2


def body(
    counts,
    random_ref, global_ref, length_ref, q_hbm, kv_hbm, cot_hbm,
    stream_hbm, gain_ref,
    kv0, kv1, kv2, kv3, qs, cs, stream, arrived, keys, values, onehot, squares,
    terms, scattered, crossed, gathered,
    ag_send, ag_recv, kv_sem, q_sem, c_sem, out_sem,
    relay_send, relay_recv, rs_send, rs_recv, z_send, z_recv, f_send, f_recv,
):
    dp_count, section_count, n = counts
    dp, section, me = lax.axis_index("dp"), lax.axis_index("section"), lax.axis_index("ctx")
    half = n // 2
    kvs = (kv0, kv1, kv2, kv3)
    right, left = lax.rem(me + 1, n), lax.rem(me + n - 1, n)

    def local_kv(h):
        copies = []
        for part in range(2):
            column = part * KVH * HD + h * HD
            copies.append(pltpu.make_async_copy(
                kv_hbm.at[0, 0, :, pl.ds(column, HD)],
                kvs[h].at[me, pl.ds(part * BLOCK, BLOCK)],
                kv_sem.at[h, part],
            ))
        return copies

    def q_copy(u):
        return pltpu.make_async_copy(
            q_hbm.at[0, 0, :, pl.ds(pl.multiple_of(u * HD, HD), HD)], qs.at[u], q_sem.at[u])

    def c_copy(u):
        return pltpu.make_async_copy(
            cot_hbm.at[0, 0, :, pl.ds(pl.multiple_of(u * HD, HD), HD)], cs.at[u], c_sem.at[u])

    def out_copy(u):
        return pltpu.make_async_copy(
            stream.at[u], stream_hbm.at[0, 0, :, pl.ds(pl.multiple_of(u * HD, HD), HD)], out_sem.at[u])

    def ring(h, d, t, last):
        sign = 1 if d == 0 else -1
        origin = lax.rem(me - sign * (t - 1) + 2 * n, n)
        place = kvs[h].at[origin, pl.ds(d * BLOCK, BLOCK)] if last else kvs[h].at[origin]
        return pltpu.make_async_remote_copy(
            src_ref=place, dst_ref=place,
            send_sem=ag_send.at[h, d, t - 1], recv_sem=ag_recv.at[h, d, t - 1],
            device_id={"ctx": right if d == 0 else left}, device_id_type=MESH)

    def ring_arrival(h, d, t, last):
        sign = 1 if d == 0 else -1
        origin = lax.rem(me - sign * t + 2 * n, n)
        place = kvs[h].at[origin, pl.ds(d * BLOCK, BLOCK)] if last else kvs[h].at[origin]
        return pltpu.make_async_remote_copy(
            src_ref=place, dst_ref=place,
            send_sem=ag_send.at[h, d, t - 1], recv_sem=ag_recv.at[h, d, t - 1],
            device_id={"ctx": right if d == 0 else left}, device_id_type=MESH)

    def ring_start(heads):
        for h in heads:
            for d in range(2):
                ring(h, d, 1, False).start()

    def ring_step(heads, t):
        @pl.when(t < half)
        def _():
            for h in heads:
                for d in range(2):
                    ring_arrival(h, d, t - 1, False).wait_recv()
                    ring(h, d, t, False).start()

        @pl.when(t == half)
        def _():
            for h in heads:
                for d in range(2):
                    ring_arrival(h, d, half - 1, False).wait_recv()
                    ring(h, d, half, True).start()

    def ring_finish(heads):
        for h in heads:
            for d in range(2):
                ring_arrival(h, d, half, True).wait_recv()

    barrier = pltpu.get_barrier_semaphore()
    for h in range(KVH):
        for copy in local_kv(h):
            copy.start()
    for target in (left, right):
        pl.semaphore_signal(barrier, inc=1, device_id={"ctx": target}, device_id_type=MESH)
    for step in (1, section_count - 1):
        pl.semaphore_signal(
            barrier, inc=1, device_id={"section": lax.rem(section + step, section_count)}, device_id_type=MESH)
    for step in range(1, dp_count):
        pl.semaphore_signal(
            barrier, inc=1, device_id={"dp": lax.rem(dp + step, dp_count)}, device_id_type=MESH)

    def start_inputs(u, carry):
        q_copy(u).start()
        c_copy(u).start()
        return carry

    lax.fori_loop(0, HEADS, start_inputs, 0)
    pl.semaphore_wait(barrier, 4 + dp_count - 1)
    for h in range(KVH):
        for copy in local_kv(h):
            copy.wait()
    ring_start((0, 1))

    ends = []
    total = 0
    for d in range(DOCS):
        total = total + length_ref[0, d]
        ends.append(total)
    lanes = lax.broadcasted_iota(jnp.int32, (BLOCK, HD), 1)
    rows = lax.broadcasted_iota(jnp.int32, (BLOCK, HD), 0)

    def doc_of(block):
        position = rows + block * BLOCK
        doc = jnp.zeros((BLOCK, HD), jnp.int32)
        for end in ends:
            doc = doc + jnp.where(position >= end, 1, 0)
        return doc

    own_hot = jnp.where(doc_of(me) == lanes, 1.0, 0.0).astype(jnp.bfloat16)
    onehot[0:BLOCK, :] = own_hot
    onehot[BLOCK:, :] = own_hot

    def gather_list(h, place):
        blocks = [
            (left, me > 0), (me, None), (right, me < n - 1),
            (global_ref[0, 0], None), (global_ref[0, 1], None),
        ]
        for r in range(RAND):
            blocks.append((random_ref[0, me, h, r], None))
        for i, (block, valid) in enumerate(blocks):
            span = pl.ds(i * BLOCK, BLOCK)
            keys[place, span, 0:HD] = kvs[h][block, 0:BLOCK, :]
            values[place, span, :] = kvs[h][block, BLOCK:, :]
            doc = doc_of(block)
            if valid is not None:
                doc = jnp.where(valid, doc, -1)
            keys[place, span, HD:] = jnp.where(doc == lanes, 0.0, -1e30).astype(jnp.bfloat16)

    def attend(pair, place):
        queries = qs[pl.ds(2 * pair, 2)].reshape(2 * BLOCK, HD)
        wide = jnp.concatenate([queries, onehot[...]], axis=1)
        scores = lax.dot_general(
            wide, keys[place], (((1,), (1,)), ((), ())), preferred_element_type=jnp.float32)
        top = jnp.max(scores, axis=-1, keepdims=True)
        weights = jnp.exp2((scores - top) * FACTOR)
        sums = jnp.sum(weights, axis=-1, keepdims=True)
        product = jnp.dot(
            weights.astype(jnp.bfloat16), values[place], preferred_element_type=jnp.float32)
        result = (product / sums).astype(jnp.bfloat16)
        stream[pl.ds(2 * pair, 2)] = result.reshape(2, BLOCK, HD)

    def relay_copy(pair):
        return pltpu.make_async_remote_copy(
            src_ref=stream.at[pl.ds(2 * pair, 2)], dst_ref=arrived.at[pl.ds(2 * pair, 2)],
            send_sem=relay_send.at[pair], recv_sem=relay_recv.at[pair],
            device_id={"section": lax.rem(section + 1, section_count)}, device_id_type=MESH)

    def relay(pair):
        span = pl.ds(2 * pair, 2)

        @pl.when(section > 0)
        def _():
            relay_copy(pair).wait_recv()
            stream[span] = (
                arrived[span].astype(jnp.float32) + stream[span].astype(jnp.float32)
            ).astype(jnp.bfloat16)

        @pl.when(section < section_count - 1)
        def _():
            relay_copy(pair).start()

        wide = stream[span].astype(jnp.float32)
        squares[...] += wide[0] * wide[0] + wide[1] * wide[1]
        out_copy(2 * pair).start()
        out_copy(2 * pair + 1).start()

    def relay_behind(i):
        behind = i - LAG * section

        @pl.when(behind >= 0)
        def _():
            relay(behind)

    squares[...] = jnp.zeros_like(squares)

    def wait_inputs(u, carry):
        q_copy(u).wait()
        c_copy(u).wait()
        return carry

    def first_phase(t, carry):
        ring_step((0, 1), t)
        return carry

    lax.fori_loop(2, half + 1, first_phase, 0)
    ring_start((2, 3))
    lax.fori_loop(0, HEADS, wait_inputs, 0)
    ring_finish((0, 1))
    gather_list(0, 0)
    gather_list(1, 1)

    def second_phase(i, carry):
        ring_step((2, 3), i + 2)
        attend(i, i // 4)
        relay_behind(i)
        return carry

    lax.fori_loop(0, PAIRS // 2, second_phase, 0)
    ring_finish((2, 3))
    gather_list(2, 0)
    gather_list(3, 1)

    def third_phase(i, carry):
        attend(i, i // 4 - 2)
        relay_behind(i)
        return carry

    lax.fori_loop(PAIRS // 2, PAIRS, third_phase, 0)

    def drain(i, carry):
        @pl.when(i - LAG * section < PAIRS)
        def _():
            relay(i - LAG * section)
        return carry

    lax.fori_loop(PAIRS, PAIRS + LAG * (section_count - 1), drain, 0)

    mean = jnp.sum(squares[...], axis=-1, keepdims=True) / (HEADS * HD)
    inverse = jnp.broadcast_to(lax.rsqrt(mean + 1e-06), (BLOCK, HD))

    def term_pair(p, carry):
        parts = []
        for j in range(2):
            u = 2 * p + j
            scaled = cs[u].astype(jnp.float32) * stream[u].astype(jnp.float32) * inverse
            parts.append(jnp.sum(scaled, axis=0, keepdims=True))
        terms[p] = jnp.concatenate(parts, axis=0) / dp_count
        return carry

    lax.fori_loop(0, PAIRS, term_pair, 0)

    width = PAIRS // dp_count

    def scatter_copy(peer):
        return pltpu.make_async_remote_copy(
            src_ref=terms.at[pl.ds(peer * width, width)], dst_ref=scattered.at[dp],
            send_sem=rs_send.at[peer], recv_sem=rs_recv.at[dp],
            device_id={"dp": peer}, device_id_type=MESH)

    def scatter_arrival(peer):
        return pltpu.make_async_remote_copy(
            src_ref=terms.at[pl.ds(peer * width, width)], dst_ref=scattered.at[peer],
            send_sem=rs_send.at[peer], recv_sem=rs_recv.at[peer],
            device_id={"dp": peer}, device_id_type=MESH)

    def cross_copy(peer):
        return pltpu.make_async_remote_copy(
            src_ref=crossed.at[me], dst_ref=crossed.at[me],
            send_sem=z_send.at[peer], recv_sem=z_recv.at[me],
            device_id={"ctx": peer}, device_id_type=MESH)

    def cross_arrival(peer):
        return pltpu.make_async_remote_copy(
            src_ref=crossed.at[peer], dst_ref=crossed.at[peer],
            send_sem=z_send.at[peer], recv_sem=z_recv.at[peer],
            device_id={"ctx": peer}, device_id_type=MESH)

    def gather_copy(peer):
        return pltpu.make_async_remote_copy(
            src_ref=gathered.at[dp], dst_ref=gathered.at[dp],
            send_sem=f_send.at[peer], recv_sem=f_recv.at[dp],
            device_id={"dp": peer}, device_id_type=MESH)

    def gather_arrival(peer):
        return pltpu.make_async_remote_copy(
            src_ref=gathered.at[peer], dst_ref=gathered.at[peer],
            send_sem=f_send.at[peer], recv_sem=f_recv.at[peer],
            device_id={"dp": peer}, device_id_type=MESH)

    def each(count, own, action):
        def one(step, carry):
            action(lax.rem(own + step, count))
            return carry
        lax.fori_loop(1, count, one, 0)

    each(dp_count, dp, lambda peer: scatter_copy(peer).start())
    scattered[dp] = terms[pl.ds(dp * width, width)]
    each(dp_count, dp, lambda peer: scatter_arrival(peer).wait_recv())
    crossed[me] = jnp.sum(scattered[...], axis=0)
    each(n, me, lambda peer: cross_copy(peer).start())
    each(n, me, lambda peer: cross_arrival(peer).wait_recv())
    gathered[dp] = jnp.sum(crossed[...], axis=0)
    each(dp_count, dp, lambda peer: gather_copy(peer).start())
    each(dp_count, dp, lambda peer: gather_arrival(peer).wait_recv())
    for p in range(PAIRS):
        for j in range(2):
            u = 2 * p + j
            gain_ref[0:1, u * HD:(u + 1) * HD] = gathered[p // width, p % width, j:j + 1, :]

    each(dp_count, dp, lambda peer: scatter_copy(peer).wait_send())
    each(n, me, lambda peer: cross_copy(peer).wait_send())
    each(dp_count, dp, lambda peer: gather_copy(peer).wait_send())

    def sent(t, carry):
        for h in range(KVH):
            for d in range(2):
                ring(h, d, t, False).wait_send()
        return carry

    lax.fori_loop(1, half, sent, 0)
    for h in range(KVH):
        for d in range(2):
            ring(h, d, half, True).wait_send()

    @pl.when(section < section_count - 1)
    def _():
        def relayed(p, carry):
            relay_copy(p).wait_send()
            return carry
        lax.fori_loop(0, PAIRS, relayed, 0)

    def written(u, carry):
        out_copy(u).wait()
        return carry

    lax.fori_loop(0, HEADS, written, 0)


def per_device(queries, keys_values, random_blocks, global_blocks, doc_lengths, cotangent):
    counts = (lax.axis_size("dp"), lax.axis_size("section"), lax.axis_size("ctx"))
    dp_count, _, n = counts
    width = PAIRS // dp_count
    dma = pltpu.SemaphoreType.DMA
    small = pl.BlockSpec(memory_space=pltpu.SMEM)
    large = pl.BlockSpec(memory_space=pl.ANY)
    unit = pltpu.VMEM((HEADS, BLOCK, HD), jnp.bfloat16)
    stream, gain = pl.pallas_call(
        functools.partial(body, counts),
        out_shape=(
            jax.ShapeDtypeStruct(queries.shape, jnp.bfloat16),
            jax.ShapeDtypeStruct((1, HEADS * HD), jnp.float32),
        ),
        in_specs=[small, small, small, large, large, large],
        out_specs=(large, pl.BlockSpec(memory_space=pltpu.VMEM)),
        scratch_shapes=[pltpu.VMEM((n, 2 * BLOCK, HD), jnp.bfloat16)] * KVH + [
            unit, unit, unit, unit,
            pltpu.VMEM((2, LISTED * BLOCK, 2 * HD), jnp.bfloat16),
            pltpu.VMEM((2, LISTED * BLOCK, HD), jnp.bfloat16),
            pltpu.VMEM((2 * BLOCK, HD), jnp.bfloat16),
            pltpu.VMEM((BLOCK, HD), jnp.float32),
            pltpu.VMEM((PAIRS, 2, HD), jnp.float32),
            pltpu.VMEM((dp_count, width, 2, HD), jnp.float32),
            pltpu.VMEM((n, width, 2, HD), jnp.float32),
            pltpu.VMEM((dp_count, width, 2, HD), jnp.float32),
            dma((KVH, 2, n // 2)), dma((KVH, 2, n // 2)), dma((KVH, 2)),
            dma((HEADS,)), dma((HEADS,)), dma((HEADS,)),
            dma((PAIRS,)), dma((PAIRS,)),
            dma((dp_count,)), dma((dp_count,)), dma((n,)), dma((n,)), dma((dp_count,)), dma((dp_count,)),
        ],
        compiler_params=pltpu.CompilerParams(
            collective_id=0, has_side_effects=True, vmem_limit_bytes=48 * 1024 * 1024),
        name="relay_attention",
    )(random_blocks, global_blocks, doc_lengths, queries, keys_values, cotangent)
    return stream, gain


def solution(mesh):
    in_specs = (
        P("section", "dp", "ctx", None),
        P("section", "dp", "ctx", None),
        P("dp", None, None, None),
        P("dp", None),
        P("dp", None),
        P("section", "dp", "ctx", None),
    )
    out_specs = (P("section", "dp", "ctx", None), P("section", None))
    return jax.shard_map(
        per_device, mesh=mesh, in_specs=in_specs, out_specs=out_specs, check_vma=False
    )
```

time: 1290 us -> 128 us (0.10); the launches traced: 1270 us -> 127 us
  blocking collectives: 977 us -> 0 us
  waiting for transfers between devices: 195 us -> 0 us
  Pallas kernels: 0 us -> 121 us
  starting transfers between devices: 29.1 us -> 0 us
  matrix products: 23.3 us -> 0 us
  between operations: 15.7 us -> 0.67 us
  local copies, waits for them, and re-layouts: 19.6 us -> 5.79 us
    psum x1 -> x0, blocking collectives: 977 us -> none  [per_device(): gain_grad = lax.psum(gradient_term, ('dp', 'ctx'))]
    psum x1 -> x0, waiting for transfers between devices: 140 us -> none  [spread(): return lax.psum(jnp.where(mine, value, jnp.zeros_like(value)), axis)]
    pallas_call x0 -> x1, Pallas kernels: none -> 121 us  [per_device(): pl.pallas_call(functools.partial(body, counts), out_shape=(jax.ShapeDtype...]
    ppermute x5 -> x0, waiting for transfers between devices: 55.1 us -> none  [the longest x3 55.1 us: passed_along(): lax.ppermute(value, axis, [(source, source + steps) for source in range(i...]
    all_to_all x1 -> x0, starting transfers between devices: 19.2 us -> none  [per_device(): lax.all_to_all(outgoing, 'ctx', split_axis=0, concat_axis=0, tiled=True)]
    dot_general x4 -> x0, matrix products: 15 us -> none  [attend_head(): jnp.einsum('gqk,kd->qgd', weights.astype(jnp.bfloat16), value_rows, prefe...]
  transfers between devices with their start and end apart: 7 -> 0, of which waited for: 4 -> 0; matrix products, arithmetic and copies ran while one was open for 1% -> 0% of each run, Pallas kernels for 0% -> 0%
where the time goes in v1:
time: 128 us; the launch traced here: 127 us
  Pallas kernels  121 us (95%)
  local copies, waits for them, and re-layouts  5.79 us (5%)
    pallas_call x1, Pallas kernels, per_device(): pl.pallas_call(functools.partial(body, counts), out_shape=(jax.ShapeDtype...  121 us
    unnamed x13, local copies, waits for them, and re-layouts  5.79 us

profile of v1, /device:TPU:7, one launch (start us, length us, event | category | flops | bytes accessed | tf_op | source)
XLA Modules:
  0.0 127.2 jit_solution(6293017898108130819)
XLA Ops:
  0.6 0.0 copy-start.4
  0.6 0.0 copy-start.3
  0.7 0.8 copy.8.random_ref
  1.5 0.0 copy-done.4
  1.5 0.0 copy-done.3
  1.5 0.0 copy-start
  1.5 1.2 copy-done
  2.7 0.0 copy-start.1
  2.7 1.2 copy-done.1
  3.9 0.0 copy-start.2
  3.9 0.9 copy-done.2
  4.9 120.8 %relay_attention.1 = (bf16[1,1,128,4096]{3,2,1,0:T(8,128)(2,1)S(1)}, f32[1,4096]{1,0:T(1,128)S(1)}) custom-call(s32[1,16,4,4]{3,2,1,0:T(4,128)S(1)} %copy.8.random_ref, s32[1,2]{1,0:T(1,128)S(1)} %copy-done.3, s32[1,4]{1,0:T(1,128)S(1)} %copy-done.4, bf16[1,1,128,4096]{3,2,1,0:T(8,128)(2,1)S(1)} %copy-done, bf16[1,1,128,1024]{3,2,1,0:T(8,128)(2,1)S(1)} %copy-done.2, ...), custom_call_target="tpu_custom_call" | custom-call | tf_op jit(solution)/shard_map/relay_attention/pallas_call | solution.py:365
  125.6 1.0 copy.11
  126.6 0.6 copy.12
Async XLA Ops:
  0.6 0.8 copy-start.4
  0.6 0.8 copy-start.3
  1.5 1.2 copy-start
  2.7 1.2 copy-start.1
  3.9 0.9 copy-start.2

commit v2 on v1

v2 whole, which is shorter than its diff:
```python
import functools
import math

import jax
import jax.numpy as jnp
from jax import lax
from jax.experimental import pallas as pl
from jax.experimental.pallas import tpu as pltpu
from jax.sharding import PartitionSpec as P

HEADS = 32
KVH = 4
HD = 128
RAND = 4
GLOBALS = 2
GROUP = 8
DOCS = 4
BLOCK = 128
LISTED = 3 + GLOBALS + RAND
PAIRS = HEADS // 2
UNIT = 4
UNITS = HEADS // UNIT
MESH = pl.DeviceIdType.MESH
FACTOR = math.log2(math.e) / math.sqrt(HD)
LAG = 1
PIECES = 2
OFFSETS = (0, 1, 3, 5)
ROWS = 2 * BLOCK // PIECES


def body(
    counts,
    random_hbm, global_hbm, length_hbm, q_hbm, kv_hbm, cot_hbm,
    stream_hbm, gain_ref,
    kv0, kv1, kv2, kv3, qs, cs, stream, arrived, keys, values, onehot, own_values, squares,
    terms, scattered, crossed, gathered,
    random_ref, global_ref, length_ref, small_sem,
    ag_send, ag_recv, kv_sem, q_sem, c_sem, out_sem,
    relay_send, relay_recv, rs_send, rs_recv, z_send, z_recv, f_send, f_recv,
):
    dp_count, section_count, n = counts
    dp, section, me = lax.axis_index("dp"), lax.axis_index("section"), lax.axis_index("ctx")
    half = n // 2
    kvs = (kv0, kv1, kv2, kv3)
    right, left = lax.rem(me + 1, n), lax.rem(me + n - 1, n)

    def local_kv(h):
        copies = []
        for part in range(2):
            column = part * KVH * HD + h * HD
            copies.append(pltpu.make_async_copy(
                kv_hbm.at[0, 0, :, pl.ds(column, HD)],
                own_values.at[h] if part else kvs[h].at[me, pl.ds(0, BLOCK)],
                kv_sem.at[h, part],
            ))
        return copies

    def q_copy(u):
        return pltpu.make_async_copy(
            q_hbm.at[0, 0, :, pl.ds(pl.multiple_of(u * HD, HD), HD)], qs.at[u], q_sem.at[u])

    def c_copy(u):
        return pltpu.make_async_copy(
            cot_hbm.at[0, 0, :, pl.ds(pl.multiple_of(u * HD, HD), HD)], cs.at[u], c_sem.at[u])

    def out_copy(u):
        return pltpu.make_async_copy(
            stream.at[u], stream_hbm.at[0, 0, :, pl.ds(pl.multiple_of(u * HD, HD), HD)], out_sem.at[u])

    def ring(h, d, t, k, landing=False):
        sign = 1 if d == 0 else -1
        origin = lax.rem(me - sign * (t if landing else t - 1) + 2 * n, n)
        place = kvs[h].at[origin, pl.ds(k * ROWS, ROWS)]
        return pltpu.make_async_remote_copy(
            src_ref=place, dst_ref=place,
            send_sem=ag_send.at[h, d, t - 1, k], recv_sem=ag_recv.at[h, d, t - 1, k],
            device_id={"ctx": right if d == 0 else left}, device_id_type=MESH)

    def order(heads, last=False):
        for h in heads:
            for k in range(PIECES):
                for d in range(2):
                    if not last or k // (PIECES // 2) == d:
                        yield h, d, k

    def ring_slot(slot):
        for h in range(KVH):
            t = slot - OFFSETS[h]
            if 1 <= t <= half:
                for _, d, k in order((h,)):
                    if t > 1:
                        ring(h, d, t - 1, k, True).wait_recv()
                    if t < half or k // (PIECES // 2) == d:
                        ring(h, d, t, k).start()

    def ring_finish(h):
        for _, d, k in order((h,), True):
            ring(h, d, half, k, True).wait_recv()

    barrier = pltpu.get_barrier_semaphore()
    for h in range(KVH):
        for copy in local_kv(h):
            copy.start()
    for target in (left, right):
        pl.semaphore_signal(barrier, inc=1, device_id={"ctx": target}, device_id_type=MESH)
    for step in (1, section_count - 1):
        pl.semaphore_signal(
            barrier, inc=1, device_id={"section": lax.rem(section + step, section_count)}, device_id_type=MESH)
    for step in range(1, dp_count):
        pl.semaphore_signal(
            barrier, inc=1, device_id={"dp": lax.rem(dp + step, dp_count)}, device_id_type=MESH)

    small = [
        pltpu.make_async_copy(source, target, small_sem.at[i])
        for i, (source, target) in enumerate(
            ((random_hbm, random_ref), (global_hbm, global_ref), (length_hbm, length_ref)))
    ]
    for copy in small:
        copy.start()

    def start_inputs(u, carry):
        q_copy(u).start()
        c_copy(u).start()
        return carry

    lax.fori_loop(0, HEADS, start_inputs, 0)
    for h in range(KVH):
        for copy in local_kv(h):
            copy.wait()
        turned = jnp.transpose(own_values[h].astype(jnp.float32))
        kvs[h][me, BLOCK:, :] = turned.astype(jnp.bfloat16)
    pl.semaphore_wait(barrier, 4 + dp_count - 1)
    ring_slot(1)

    for copy in small:
        copy.wait()
    ends = []
    total = 0
    for d in range(DOCS):
        total = total + length_ref[0, d]
        ends.append(total)
    lanes = lax.broadcasted_iota(jnp.int32, (BLOCK, HD), 1)
    rows = lax.broadcasted_iota(jnp.int32, (BLOCK, HD), 0)

    def doc_of(block):
        position = rows + block * BLOCK
        doc = jnp.zeros((BLOCK, HD), jnp.int32)
        for end in ends:
            doc = doc + jnp.where(position >= end, 1, 0)
        return doc

    own_hot = jnp.where(doc_of(me) == lanes, 1.0, 0.0).astype(jnp.bfloat16)
    for j in range(UNIT):
        onehot[j * BLOCK:(j + 1) * BLOCK, :] = own_hot

    def listed(h):
        blocks = [
            (left, me > 0), (me, None), (right, me < n - 1),
            (global_ref[0, 0], None), (global_ref[0, 1], None),
        ]
        for r in range(RAND):
            blocks.append((random_ref[0, h, r, me], None))
        return [(pl.ds(i * BLOCK, BLOCK),) + block for i, block in enumerate(blocks)]

    def mask_list(h):
        for span, block, valid in listed(h):
            doc = doc_of(block)
            if valid is not None:
                doc = jnp.where(valid, doc, -1)
            keys[h, span, HD:] = jnp.where(doc == lanes, 0.0, -1e30).astype(jnp.bfloat16)

    def gather_list(h):
        for span, block, _ in listed(h):
            keys[h, span, 0:HD] = kvs[h][block, 0:BLOCK, :]
            values[h, :, span] = kvs[h][block, BLOCK:, :]

    def attend(i):
        h = i // (UNITS // KVH)
        queries = qs[pl.ds(UNIT * i, UNIT)].reshape(UNIT * BLOCK, HD)
        wide = jnp.concatenate([queries, onehot[...]], axis=1)
        scores = lax.dot_general(
            keys[h], wide, (((1,), (1,)), ((), ())), preferred_element_type=jnp.float32)
        top = jnp.max(scores, axis=0, keepdims=True)
        weights = jnp.exp2((scores - top) * FACTOR)
        sums = jnp.sum(weights, axis=0, keepdims=True)
        product = jnp.dot(
            values[h], weights.astype(jnp.bfloat16), preferred_element_type=jnp.float32)
        result = jnp.transpose(product / sums).astype(jnp.bfloat16)
        stream[pl.ds(UNIT * i, UNIT)] = result.reshape(UNIT, BLOCK, HD)

    def relay_copy(u):
        return pltpu.make_async_remote_copy(
            src_ref=stream.at[u], dst_ref=arrived.at[u],
            send_sem=relay_send.at[u], recv_sem=relay_recv.at[u],
            device_id={"section": lax.rem(section + 1, section_count)}, device_id_type=MESH)

    def relay(i):
        for j in range(UNIT):
            u = UNIT * i + j

            @pl.when(section > 0)
            def _():
                relay_copy(u).wait_recv()
                stream[u] = (
                    arrived[u].astype(jnp.float32) + stream[u].astype(jnp.float32)
                ).astype(jnp.bfloat16)

            @pl.when(section < section_count - 1)
            def _():
                relay_copy(u).start()

            wide = stream[u].astype(jnp.float32)
            squares[...] += wide * wide
            out_copy(u).start()

    def relay_behind(i):
        behind = i - LAG * section

        @pl.when(behind >= 0)
        def _():
            relay(behind)

    squares[...] = jnp.zeros_like(squares)
    for h in range(KVH):
        mask_list(h)

    def wait_inputs(u, carry):
        q_copy(u).wait()
        c_copy(u).wait()
        return carry

    for slot in range(2, half + 1):
        ring_slot(slot)
        if slot == max(2, half - 1):
            lax.fori_loop(0, HEADS, wait_inputs, 0)

    units_of_head = UNITS // KVH

    def step(i, carry):
        for h in range(KVH):
            @pl.when(i == h * units_of_head)
            def _():
                ring_finish(h)
                gather_list(h)
        for late in range(OFFSETS[-1]):
            @pl.when(i == late)
            def _():
                ring_slot(half + 1 + late)
        attend(i)
        relay_behind(i)
        return carry

    lax.fori_loop(0, UNITS, step, 0)

    def drain(i, carry):
        @pl.when(i - LAG * section < UNITS)
        def _():
            relay(i - LAG * section)
        return carry

    lax.fori_loop(UNITS, UNITS + LAG * (section_count - 1), drain, 0)

    mean = jnp.sum(squares[...], axis=-1, keepdims=True) / (HEADS * HD)
    inverse = jnp.broadcast_to(lax.rsqrt(mean + 1e-06), (BLOCK, HD))

    def term_pair(p, carry):
        parts = []
        for j in range(2):
            u = 2 * p + j
            scaled = cs[u].astype(jnp.float32) * stream[u].astype(jnp.float32) * inverse
            parts.append(jnp.sum(scaled, axis=0, keepdims=True))
        terms[p] = jnp.concatenate(parts, axis=0) / dp_count
        return carry

    lax.fori_loop(0, PAIRS, term_pair, 0)

    width = PAIRS // dp_count

    def scatter_copy(peer):
        return pltpu.make_async_remote_copy(
            src_ref=terms.at[pl.ds(peer * width, width)], dst_ref=scattered.at[dp],
            send_sem=rs_send.at[peer], recv_sem=rs_recv.at[dp],
            device_id={"dp": peer}, device_id_type=MESH)

    def scatter_arrival(peer):
        return pltpu.make_async_remote_copy(
            src_ref=terms.at[pl.ds(peer * width, width)], dst_ref=scattered.at[peer],
            send_sem=rs_send.at[peer], recv_sem=rs_recv.at[peer],
            device_id={"dp": peer}, device_id_type=MESH)

    def cross_copy(peer):
        return pltpu.make_async_remote_copy(
            src_ref=crossed.at[me], dst_ref=crossed.at[me],
            send_sem=z_send.at[peer], recv_sem=z_recv.at[me],
            device_id={"ctx": peer}, device_id_type=MESH)

    def cross_arrival(peer):
        return pltpu.make_async_remote_copy(
            src_ref=crossed.at[peer], dst_ref=crossed.at[peer],
            send_sem=z_send.at[peer], recv_sem=z_recv.at[peer],
            device_id={"ctx": peer}, device_id_type=MESH)

    def gather_copy(peer):
        return pltpu.make_async_remote_copy(
            src_ref=gathered.at[dp], dst_ref=gathered.at[dp],
            send_sem=f_send.at[peer], recv_sem=f_recv.at[dp],
            device_id={"dp": peer}, device_id_type=MESH)

    def gather_arrival(peer):
        return pltpu.make_async_remote_copy(
            src_ref=gathered.at[peer], dst_ref=gathered.at[peer],
            send_sem=f_send.at[peer], recv_sem=f_recv.at[peer],
            device_id={"dp": peer}, device_id_type=MESH)

    def far_first(count, chip):
        return sorted(range(1, count), key=lambda step: -min(step // chip, (count - step) // chip))

    def each(count, chip, own, action):
        for step in far_first(count, chip):
            action(lax.rem(own + step, count))

    each(dp_count, 2, dp, lambda peer: scatter_copy(peer).start())
    scattered[dp] = terms[pl.ds(dp * width, width)]

    def written(u, carry):
        out_copy(u).wait()
        return carry

    lax.fori_loop(0, HEADS, written, 0)
    each(dp_count, 2, dp, lambda peer: scatter_arrival(peer).wait_recv())
    crossed[me] = jnp.sum(scattered[...], axis=0)
    each(n, 1, me, lambda peer: cross_copy(peer).start())

    def sent(t, carry):
        for h, d, k in order(range(KVH)):
            ring(h, d, t, k).wait_send()
        return carry

    lax.fori_loop(1, half, sent, 0)
    for h, d, k in order(range(KVH), True):
        ring(h, d, half, k).wait_send()

    @pl.when(section < section_count - 1)
    def _():
        def relayed(u, carry):
            relay_copy(u).wait_send()
            return carry
        lax.fori_loop(0, HEADS, relayed, 0)

    each(dp_count, 2, dp, lambda peer: scatter_copy(peer).wait_send())
    each(n, 1, me, lambda peer: cross_arrival(peer).wait_recv())
    gathered[dp] = jnp.sum(crossed[...], axis=0)
    each(dp_count, 2, dp, lambda peer: gather_copy(peer).start())
    each(n, 1, me, lambda peer: cross_copy(peer).wait_send())
    each(dp_count, 2, dp, lambda peer: gather_arrival(peer).wait_recv())
    for p in range(PAIRS):
        for j in range(2):
            u = 2 * p + j
            gain_ref[0:1, u * HD:(u + 1) * HD] = gathered[p // width, p % width, j:j + 1, :]
    each(dp_count, 2, dp, lambda peer: gather_copy(peer).wait_send())


def per_device(queries, keys_values, random_blocks, global_blocks, doc_lengths, cotangent):
    counts = (lax.axis_size("dp"), lax.axis_size("section"), lax.axis_size("ctx"))
    dp_count, _, n = counts
    width = PAIRS // dp_count
    dma = pltpu.SemaphoreType.DMA
    held = pl.BlockSpec(memory_space=pltpu.HBM)
    large = pl.BlockSpec(memory_space=pl.ANY)
    unit = pltpu.VMEM((HEADS, BLOCK, HD), jnp.bfloat16)
    stream, gain = pl.pallas_call(
        functools.partial(body, counts),
        out_shape=(
            jax.ShapeDtypeStruct(queries.shape, jnp.bfloat16),
            jax.ShapeDtypeStruct((1, HEADS * HD), jnp.float32),
        ),
        in_specs=[held] * 6,
        out_specs=(large, pl.BlockSpec(memory_space=pltpu.VMEM)),
        scratch_shapes=[pltpu.VMEM((n, 2 * BLOCK, HD), jnp.bfloat16)] * KVH + [
            unit, unit, unit, unit,
            pltpu.VMEM((KVH, LISTED * BLOCK, 2 * HD), jnp.bfloat16),
            pltpu.VMEM((KVH, HD, LISTED * BLOCK), jnp.bfloat16),
            pltpu.VMEM((UNIT * BLOCK, HD), jnp.bfloat16),
            pltpu.VMEM((KVH, BLOCK, HD), jnp.bfloat16),
            pltpu.VMEM((BLOCK, HD), jnp.float32),
            pltpu.VMEM((PAIRS, 2, HD), jnp.float32),
            pltpu.VMEM((dp_count, width, 2, HD), jnp.float32),
            pltpu.VMEM((n, width, 2, HD), jnp.float32),
            pltpu.VMEM((dp_count, width, 2, HD), jnp.float32),
            pltpu.SMEM((1, KVH, RAND, n), jnp.int32),
            pltpu.SMEM((1, GLOBALS), jnp.int32),
            pltpu.SMEM((1, DOCS), jnp.int32),
            dma((3,)),
            dma((KVH, 2, n // 2, PIECES)), dma((KVH, 2, n // 2, PIECES)), dma((KVH, 2)),
            dma((HEADS,)), dma((HEADS,)), dma((HEADS,)),
            dma((HEADS,)), dma((HEADS,)),
            dma((dp_count,)), dma((dp_count,)), dma((n,)), dma((n,)), dma((dp_count,)), dma((dp_count,)),
        ],
        compiler_params=pltpu.CompilerParams(
            collective_id=0, has_side_effects=True, vmem_limit_bytes=67043328),
        name="relay_attention",
    )(jnp.transpose(random_blocks, (0, 2, 3, 1)), global_blocks, doc_lengths, queries, keys_values, cotangent)
    return stream, gain


def solution(mesh):
    in_specs = (
        P("section", "dp", "ctx", None),
        P("section", "dp", "ctx", None),
        P("dp", None, None, None),
        P("dp", None),
        P("dp", None),
        P("section", "dp", "ctx", None),
    )
    out_specs = (P("section", "dp", "ctx", None), P("section", None))
    return jax.shard_map(
        per_device, mesh=mesh, in_specs=in_specs, out_specs=out_specs, check_vma=False
    )
```

time: 128 us -> 114 us (0.89)
  Pallas kernels: 121 us -> 110 us
  local copies, waits for them, and re-layouts: 5.79 us -> 2.9 us
    pallas_call x1, Pallas kernels: 121 us -> 110 us  [per_device(): pl.pallas_call(functools.partial(body, counts), out_shape=(jax.ShapeDtype...]
    unnamed x13 -> x4, local copies, waits for them, and re-layouts: 5.79 us -> 2.9 us
where the time goes in v2:
time: 114 us
  Pallas kernels  110 us (96%)
  local copies, waits for them, and re-layouts  2.9 us (3%)
    pallas_call x1, Pallas kernels, per_device(): pl.pallas_call(functools.partial(body, counts), out_shape=(jax.ShapeDtype...  110 us
    unnamed x4, local copies, waits for them, and re-layouts  2.9 us

profile of v2, /device:TPU:7, one launch (start us, length us, event | category | flops | bytes accessed | tf_op | source)
XLA Modules:
  0.0 113.9 jit_solution(9078046214886833596)
XLA Ops:
  0.6 110.3 %relay_attention.1 = (bf16[1,1,128,4096]{3,2,1,0:T(8,128)(2,1)}, f32[1,4096]{1,0:T(1,128)}) custom-call(s32[1,4,4,16]{3,2,1,0:T(4,128)} %bitcast.1, s32[1,2]{1,0:T(1,128)} %global_hbm.1, s32[1,4]{1,0:T(1,128)} %length_hbm.1, bf16[1,1,128,4096]{3,2,1,0:T(8,128)(2,1)} %q_hbm.1, bf16[1,1,128,1024]{3,2,1,0:T(8,128)(2,1)} %kv_hbm.1, bf16[1,1,128,4096]{3,2,1,0:T(8,128)(2,1)} %cot_hbm.1), custom_call_target="tpu_custom_call" | custom-call | tf_op jit(solution)/shard_map/relay_attention/pallas_call | solution.py:371
  111.0 0.0 copy-start
  111.0 2.3 %copy.10 = bf16[1,1,128,4096]{3,2,1,0:T(8,128)(2,1)} copy(bf16[1,1,128,4096]{3,2,1,0:T(8,128)(2,1)} %get-tuple-element.4) | data formatting | bytes 2097152
  113.3 0.0 copy-done
  113.3 0.6 copy.11
Async XLA Ops:
  111.0 2.3 %copy-start = (f32[1,4096]{1,0:T(1,128)S(1)}, f32[1,4096]{1,0:T(1,128)}, u32[]{:S(2)}) copy-start(f32[1,4096]{1,0:T(1,128)} %get-tuple-element.5) | copy-start | bytes 49156

commit v3 on v2

--- a/solution.py
+++ b/solution.py
@@ -263,17 +263,6 @@
     mean = jnp.sum(squares[...], axis=-1, keepdims=True) / (HEADS * HD)
     inverse = jnp.broadcast_to(lax.rsqrt(mean + 1e-06), (BLOCK, HD))
 
-    def term_pair(p, carry):
-        parts = []
-        for j in range(2):
-            u = 2 * p + j
-            scaled = cs[u].astype(jnp.float32) * stream[u].astype(jnp.float32) * inverse
-            parts.append(jnp.sum(scaled, axis=0, keepdims=True))
-        terms[p] = jnp.concatenate(parts, axis=0) / dp_count
-        return carry
-
-    lax.fori_loop(0, PAIRS, term_pair, 0)
-
     width = PAIRS // dp_count
 
     def scatter_copy(peer):
@@ -319,7 +308,28 @@
         for step in far_first(count, chip):
             action(lax.rem(own + step, count))
 
-    each(dp_count, 2, dp, lambda peer: scatter_copy(peer).start())
+    def peer_at(i):
+        middle = dp_count // 2
+        step = jnp.where(lax.rem(i, 2) == 1, middle - (i + 1) // 2, middle + i // 2)
+        return lax.rem(dp + step, dp_count)
+
+    def term_piece(i, carry):
+        first = peer_at(i) * width
+        for w in range(width):
+            p = first + w
+            parts = []
+            for j in range(2):
+                u = 2 * p + j
+                scaled = cs[u].astype(jnp.float32) * stream[u].astype(jnp.float32) * inverse
+                parts.append(jnp.sum(scaled, axis=0, keepdims=True))
+            terms[p] = jnp.concatenate(parts, axis=0) / dp_count
+
+        @pl.when(i > 0)
+        def _():
+            scatter_copy(peer_at(i - 1)).start()
+        return carry
+
+    lax.fori_loop(0, dp_count, term_piece, 0)
     scattered[dp] = terms[pl.ds(dp * width, width)]
 
     def written(u, carry):

time: 114 us -> 114 us (level)
  no operation moved by 1% of the time
where the time goes in v3:
time: 114 us; the launch traced here: 113 us
  Pallas kernels  110 us (96%)
  local copies, waits for them, and re-layouts  2.9 us (3%)
    pallas_call x1, Pallas kernels, per_device(): pl.pallas_call(functools.partial(body, counts), out_shape=(jax.ShapeDtype...  110 us
    unnamed x4, local copies, waits for them, and re-layouts  2.9 us

profile of v3, /device:TPU:7, one launch (start us, length us, event | category | flops | bytes accessed | tf_op | source)
XLA Modules:
  0.0 113.3 jit_solution(5165861126966042978)
XLA Ops:
  0.6 109.7 %relay_attention.1 = (bf16[1,1,128,4096]{3,2,1,0:T(8,128)(2,1)}, f32[1,4096]{1,0:T(1,128)}) custom-call(s32[1,4,4,16]{3,2,1,0:T(4,128)} %bitcast.1, s32[1,2]{1,0:T(1,128)} %global_hbm.1, s32[1,4]{1,0:T(1,128)} %length_hbm.1, bf16[1,1,128,4096]{3,2,1,0:T(8,128)(2,1)} %q_hbm.1, bf16[1,1,128,1024]{3,2,1,0:T(8,128)(2,1)} %kv_hbm.1, bf16[1,1,128,4096]{3,2,1,0:T(8,128)(2,1)} %cot_hbm.1), custom_call_target="tpu_custom_call" | custom-call | tf_op jit(solution)/shard_map/relay_attention/pallas_call | solution.py:381
  110.4 0.0 copy-start
  110.4 2.3 %copy.10 = bf16[1,1,128,4096]{3,2,1,0:T(8,128)(2,1)} copy(bf16[1,1,128,4096]{3,2,1,0:T(8,128)(2,1)} %get-tuple-element.4) | data formatting | bytes 2097152
  112.7 0.0 copy-done
  112.7 0.6 copy.11
Async XLA Ops:
  110.4 2.3 %copy-start = (f32[1,4096]{1,0:T(1,128)S(1)}, f32[1,4096]{1,0:T(1,128)}, u32[]{:S(2)}) copy-start(f32[1,4096]{1,0:T(1,128)} %get-tuple-element.5) | copy-start | bytes 49156
